TPU v7x, 32 devices: a whole 2x2x4 slice. The times are simulated.
32 devices in a mesh: zone: 8 (over z, y), band: 4 (over x, core).
Axes of the slice: x: 2, y: 2, z: 4, core: 2. Of those that a mesh axis runs over, the one named last changes fastest.
Arguments:
- pixels: float32 [4096, 32, 128], P(('zone', 'band')), may hold values from -6 to 6
- inv_var: float32 [4096, 32, 128], P(('zone', 'band')), may hold values from 0.25 to 4
- tile_offset: float32 [2, 4096], P(None, ('zone', 'band')), may hold values from 12 to 116, as said below
- psf_amp: float32 [3, 4096], P(None, ('zone', 'band')), may hold values from 0.3 to 1
- psf_sigma: float32 [3, 4096], P(None, ('zone', 'band')), may hold values from 0.9 to 2
- tile_blob: int32 [4096], P(('zone', 'band')), may hold values from 0 to 511, as said below
- tile_band: int32 [4096], P(('zone', 'band')), may hold values from 0 to 2
- source_pos: float32 [2, 4096], P(None, 'zone'), may hold values from -5.3 to 5.3
- edge_rows: int32 [1024], P('zone'), may hold values from 0 to 511, as said below
- blob_members: int32 [512, 16], P('zone'), may hold values from 0 to 639, as said below
- sources_per_blob: int32 [512], P('zone'), may hold values from 1 to 16, as said below
Outputs:
- fluxes: float32 [3, 4096], P(None, 'zone')
Inputs may be any that keep to these rules, and one draw needn't show every extreme that they name: `tile_blob`: blob b lies in zone b // 64. Of one device's 128 tiles at most 32 cover blobs of one zone, and in every draw some zone receives exactly 32 tiles from every device of each band group. `edge_rows`: per zone, 64 lower edge rows then 64 upper edge rows, local row numbers, all 128 distinct. `blob_members`: slots at or beyond the blob's count hold 0. Every source is the live member of exactly one blob: a zone's lower edge rows belong to blobs of the previous zone and its upper edge rows to blobs of the next zone, except the first zone's lower and the last zone's upper rows, which stay in their own zone; the first zone never names the first 64 entries, the last zone never the last 64. `sources_per_blob`: the counts of one zone sum to 512; in every zone some blob has 16. `tile_offset`: row offsets lie within 12 to 20.
All inputs are finite; a program needn't handle non-finite values.
Results may differ from a plain program's by a relative error of at most 0.0003.
Values sent between devices are 32-bit elements; how exact they have to be, the bound alone decides.
A program may use at most 64 MiB of HBM per device.

v0:
```python
import jax
import jax.numpy as jnp
from jax import lax
from jax.sharding import PartitionSpec as P

FILTER_BANDS = 3
MAX_SOURCES = 16


HIGH = lax.Precision.HIGHEST
PRIOR = 1.0


def extended_2(block, sides, width):
    for axis, dim in sides:
        count = lax.axis_size(axis)
        forward = [(i, i + 1) for i in range(count - 1)]
        backward = [(target, source) for source, target in forward]
        low = lax.ppermute(
            lax.slice_in_dim(block, block.shape[dim] - width, None, axis=dim), axis, forward
        )
        high = lax.ppermute(lax.slice_in_dim(block, 0, width, axis=dim), axis, backward)
        block = jnp.concatenate([low, block, high], axis=dim)
    return block


def terms_per_tile(
    tile_image_pixels,
    tile_weight_pixels,
    pixel_shift,
    source_amplitude,
    profile_widths,
    source_location,
    slot_alive_flags,
):
    pixel_rows = jnp.arange(tile_image_pixels.shape[0]).astype(jnp.float32)
    pixel_cols = jnp.arange(tile_image_pixels.shape[1]).astype(jnp.float32)
    inverse_spread = 0.5 / (profile_widths * profile_widths)
    row_displacement = pixel_rows[None, :] - pixel_shift[0] - source_location[0][:, None]
    delta_col = pixel_cols[None, :] - pixel_shift[1] - source_location[1][:, None]
    row_profile = jnp.exp(
        -inverse_spread[None, :, None] * (row_displacement * row_displacement)[:, None, :]
    ) * (source_amplitude[None, :, None] * slot_alive_flags[:, None, None])
    profile_col = jnp.exp(-inverse_spread[None, :, None] * (delta_col * delta_col)[:, None, :])
    rendered = jnp.sum(row_profile[:, :, :, None] * profile_col[:, :, None, :], axis=1).reshape(
        row_profile.shape[0], -1
    )
    weighted = rendered * tile_weight_pixels.reshape(1, -1)
    normal = jnp.einsum("sp,tp->st", weighted, rendered, precision=HIGH)
    projected = jnp.einsum("sp,p->s", weighted, tile_image_pixels.reshape(-1), precision=HIGH)
    return (normal, projected)


def stacked_terms(
    image_stack,
    pixel_weights,
    pixel_shifts,
    source_amplitudes,
    profile_widths,
    source_locations,
    slot_alive_flags,
):

    def single_tile(packed):
        return terms_per_tile(*packed)

    return lax.map(
        single_tile,
        (
            image_stack,
            pixel_weights,
            pixel_shifts,
            source_amplitudes,
            profile_widths,
            source_locations,
            slot_alive_flags,
        ),
        batch_size=8,
    )


def send_index(tile_blob, zone_count, blob_device_table, capacity):
    dest_zone = tile_blob // blob_device_table
    onehot = (dest_zone[:, None] == jnp.arange(zone_count, dtype=jnp.int32)[None, :]).astype(
        jnp.int32
    )
    earlier = jnp.cumsum(onehot, axis=0) - onehot
    slot_index = jnp.sum(earlier * onehot, axis=1)
    return dest_zone * capacity + slot_index


def accumulate(normal, projected, labels, blob_device_table):
    target_code = labels[:, 0] * FILTER_BANDS + labels[:, 1]
    targets = jnp.arange(blob_device_table * FILTER_BANDS).astype(jnp.float32)
    selector = (target_code[:, None] == targets[None, :]).astype(jnp.float32)
    order_n = normal.shape[1]
    matrices = jnp.einsum(
        "nq,nm->qm", selector, normal.reshape(normal.shape[0], -1), precision=HIGH
    ).reshape(-1, order_n, order_n)
    vectors = jnp.einsum("nq,ns->qs", selector, projected, precision=HIGH)
    return (matrices, vectors)


def solve_blocks(normal, vector):
    order_n = normal.shape[1]
    matrix = jnp.transpose(normal, (1, 2, 0))
    source = jnp.transpose(vector)
    factor = {}
    for column in range(order_n):
        diagonal = matrix[column, column] + PRIOR
        for inner_k in range(column):
            diagonal = diagonal - factor[column, inner_k] * factor[column, inner_k]
        pivot_root = jnp.sqrt(diagonal)
        factor[column, column] = pivot_root
        for row_index in range(column + 1, order_n):
            entry_val = matrix[row_index, column]
            for inner_k in range(column):
                entry_val = entry_val - factor[row_index, inner_k] * factor[column, inner_k]
            factor[row_index, column] = entry_val / pivot_root
    forward = []
    for row_index in range(order_n):
        entry_val = source[row_index]
        for inner_k in range(row_index):
            entry_val = entry_val - factor[row_index, inner_k] * forward[inner_k]
        forward.append(entry_val / factor[row_index, row_index])
    result_rows = [None] * order_n
    for row_index in reversed(range(order_n)):
        entry_val = forward[row_index]
        for inner_k in range(row_index + 1, order_n):
            entry_val = entry_val - factor[inner_k, row_index] * result_rows[inner_k]
        result_rows[row_index] = entry_val / factor[row_index, row_index]
    return jnp.transpose(jnp.stack(result_rows))


def on_device(
    pixels,
    inv_var,
    tile_offset,
    psf_amp,
    psf_sigma,
    tile_blob,
    tile_band,
    source_pos,
    edge_rows,
    blob_members,
    sources_per_blob,
):
    zone_count = lax.axis_size("zone")
    blob_device_table = sources_per_blob.shape[0]
    src_dev = source_pos.shape[1]
    edge_width = edge_rows.shape[0] // 2
    tile_count = pixels.shape[0]
    capacity = max(2, (2 * tile_count + zone_count - 1) // zone_count)
    slots_all = zone_count * capacity
    lower_rows = edge_rows[:edge_width]
    upper_rows = edge_rows[edge_width:]
    rim_rows = jnp.concatenate([source_pos[:, lower_rows], source_pos[:, upper_rows]], axis=1)
    framed = extended_2(rim_rows, (("zone", 1),), edge_width)
    extended = jnp.concatenate(
        [framed[:, :edge_width], source_pos, framed[:, 3 * edge_width :]], axis=1
    )
    slot_alive_flags = (
        jnp.arange(MAX_SOURCES, dtype=jnp.int32)[None, :] < sources_per_blob[:, None]
    ).astype(jnp.float32)
    member_pos = jnp.transpose(extended[:, blob_members], (1, 0, 2))
    positions_flat = send_index(tile_blob, zone_count, blob_device_table, capacity)
    labels = jnp.stack(
        [(tile_blob % blob_device_table).astype(jnp.float32), tile_band.astype(jnp.float32)], axis=1
    )
    asked = (
        jnp.zeros((slots_all,), jnp.int32)
        .at[positions_flat]
        .set(tile_blob % blob_device_table)
        .reshape(zone_count, capacity)
    )
    wanted = lax.all_to_all(asked, "zone", split_axis=0, concat_axis=0, tiled=True)
    found_pos = member_pos[wanted]
    found_live = slot_alive_flags[wanted]
    reply_pos = lax.all_to_all(found_pos, "zone", split_axis=0, concat_axis=0, tiled=True)
    reply_live = lax.all_to_all(found_live, "zone", split_axis=0, concat_axis=0, tiled=True)
    tile_pos = reply_pos.reshape(slots_all, 2, MAX_SOURCES)[positions_flat]
    tile_live = reply_live.reshape(slots_all, MAX_SOURCES)[positions_flat]
    normal_own, projected_own = stacked_terms(
        pixels, inv_var, tile_offset.T, psf_amp.T, psf_sigma.T, tile_pos, tile_live
    )
    normal_buf = (
        jnp.zeros((slots_all, MAX_SOURCES, MAX_SOURCES), jnp.float32)
        .at[positions_flat]
        .set(normal_own)
        .reshape(zone_count, capacity, MAX_SOURCES, MAX_SOURCES)
    )
    projected_buf = (
        jnp.zeros((slots_all, MAX_SOURCES), jnp.float32)
        .at[positions_flat]
        .set(projected_own)
        .reshape(zone_count, capacity, MAX_SOURCES)
    )
    labels_buf = (
        jnp.zeros((slots_all, 2), jnp.float32)
        .at[positions_flat]
        .set(labels)
        .reshape(zone_count, capacity, 2)
    )
    normal_got, projected_got, labels_got = (
        lax.all_to_all(normal_buf, "zone", split_axis=0, concat_axis=0, tiled=True),
        lax.all_to_all(projected_buf, "zone", split_axis=0, concat_axis=0, tiled=True),
        lax.all_to_all(labels_buf, "zone", split_axis=0, concat_axis=0, tiled=True),
    )
    items_got = normal_got.shape[0] * normal_got.shape[1]
    matrices, vectors = accumulate(
        normal_got.reshape(items_got, MAX_SOURCES, MAX_SOURCES),
        projected_got.reshape(items_got, MAX_SOURCES),
        labels_got.reshape(items_got, 2),
        blob_device_table,
    )
    matrices, vectors = lax.psum((matrices, vectors), "band")
    solved_fluxes = solve_blocks(matrices, vectors)
    value_entries = (
        solved_fluxes.reshape(blob_device_table, FILTER_BANDS, MAX_SOURCES)
        * slot_alive_flags[:, None, :]
    )
    spread = jnp.transpose(value_entries, (1, 0, 2)).reshape(FILTER_BANDS, -1)
    flux_ext = (
        jnp.zeros((FILTER_BANDS, src_dev + 2 * edge_width), jnp.float32)
        .at[:, blob_members.reshape(-1)]
        .add(spread)
    )
    rim_back = jnp.concatenate(
        [flux_ext[:, :edge_width], flux_ext[:, edge_width + src_dev :]], axis=1
    )
    returned = extended_2(rim_back, (("zone", 1),), edge_width)
    own_flux = flux_ext[:, edge_width : edge_width + src_dev]
    own_flux = own_flux.at[:, lower_rows].add(returned[:, :edge_width])
    own_flux = own_flux.at[:, upper_rows].add(returned[:, 3 * edge_width :])
    return own_flux


def solution(mesh):
    return jax.shard_map(
        on_device,
        mesh=mesh,
        in_specs=(
            P(("zone", "band"), None, None),
            P(("zone", "band"), None, None),
            P(None, ("zone", "band")),
            P(None, ("zone", "band")),
            P(None, ("zone", "band")),
            P(("zone", "band")),
            P(("zone", "band")),
            P(None, "zone"),
            P("zone"),
            P("zone", None),
            P("zone"),
        ),
        out_specs=P(None, "zone"),
        check_vma=False,
    )
```

profile of v0, /device:TPU:0, one launch (start us, length us, event | category | flops | bytes accessed | tf_op | source)
XLA Modules:
  0.0 382.4 jit_solution(5451843992659567161)
XLA Ops:
  9.3 7.3 %all-to-all-start.1 = ((s32[8,1,32]{2,1,0:T(1,128)}), s32[8,1,32]{2,1,0:T(1,128)S(1)}, u32[]{:S(2)}, u32[]{:S(2)}) async-start(s32[8,1,32]{2,1,0:T(1,128)} %all_to_all.24), calls=%async_computation.1 | async-start | bytes 8192 | tf_op jit(solution)/shard_map/all_to_all | solution.py:176
  18.9 3.9 %collective-permute-start = (f32[2,64]{0,1:T(8,128)S(1)}, f32[2,64]{0,1:T(8,128)S(1)}, u32[]{:S(2)}, u32[]{:S(2)}) collective-permute-start(f32[2,64]{0,1:T(8,128)S(1)} %bitcast.1988), channel_id=1, source_target_pairs={{0,4},{4,8},{8,12},{12,16},{16,20},{20,24},{24,28},{1,5},{5,9},{9,... | collective-permute-start | bytes 1544 | tf_op jit(solution)/shard_map/ppermute | solution.py:19
  33.5 6.6 %all-to-all-start.3 = ((f32[8,1,512]{2,1,0:T(1,128)}), f32[8,1,512]{2,1,0:T(1,128)S(1)}, u32[]{:S(2)}, u32[]{:S(2)}) async-start(f32[8,1,512]{2,1,0:T(1,128)} %reshape.21247), calls=%async_computation.3 | async-start | bytes 32768 | tf_op jit(solution)/shard_map/all_to_all | solution.py:180
  40.2 2.8 gather_fusion.2
  46.7 4.6 %all-to-all-start.2 = ((f32[8,1,1024]{2,1,0:T(1,128)}), f32[8,1,1024]{2,1,0:T(1,128)S(1)}, u32[]{:S(2)}, u32[]{:S(2)}) async-start(f32[8,1,1024]{2,1,0:T(1,128)} %reshape.21245), calls=%async_computation.2 | async-start | bytes 65536 | tf_op jit(solution)/shard_map/all_to_all | solution.py:179
  53.3 4.8 %all-to-all-done.2 = f32[8,1,1024]{2,1,0:T(1,128)S(1)} async-done(((f32[8,1,1024]{2,1,0:T(1,128)}), f32[8,1,1024]{2,1,0:T(1,128)S(1)}, u32[]{:S(2)}, u32[]{:S(2)}) %all-to-all-start.2) | async-done | bytes 32800 | tf_op jit(solution)/shard_map/all_to_all | solution.py:179
  58.0 3.3 all-to-all-start
  63.0 210.3 %while.12 = (s32[]{:T(128)}, f32[16,8,16,16]{3,2,1,0:T(8,128)S(1)}, f32[16,8,16]{2,1,0:T(8,128)S(1)}, f32[16,8,3]{1,0,2:T(8,128)S(1)}, f32[16,8,2]{1,0,2:T(8,128...) while((s32[]{:T(128)}, f32[16,8,16,16]{3,2,1,0:T(8,128)S(1)}, ...), condition=%wide.region_6.7_spmd, body=%wide.region_4.6_spmd.sunk | while | flops 110741352 | bytes 14517353 | solution.py:67
  64.1 3.5 multiply_reduce_fusion.2
  70.4 3.2 fusion.492
  73.6 2.6 fusion.493
  77.2 3.5 multiply_reduce_fusion.2
  83.6 3.2 fusion.492
  86.7 2.6 fusion.493
  90.4 3.5 multiply_reduce_fusion.2
  96.7 3.2 fusion.492
  99.9 2.6 fusion.493
  103.5 3.5 multiply_reduce_fusion.2
  109.8 3.2 fusion.492
  113.0 2.6 fusion.493
  116.7 3.5 multiply_reduce_fusion.2
  123.0 3.2 fusion.492
  126.1 2.6 fusion.493
  129.8 3.5 multiply_reduce_fusion.2
  136.1 3.2 fusion.492
  139.3 2.6 fusion.493
  142.9 3.5 multiply_reduce_fusion.2
  149.3 3.2 fusion.492
  152.4 2.6 fusion.493
  156.1 3.5 multiply_reduce_fusion.2
  162.4 3.2 fusion.492
  165.6 2.6 fusion.493
  169.2 3.5 multiply_reduce_fusion.2
  175.5 3.2 fusion.492
  178.7 2.6 fusion.493
  182.4 3.5 multiply_reduce_fusion.2
  188.7 3.2 fusion.492
  191.8 2.6 fusion.493
  195.5 3.5 multiply_reduce_fusion.2
  201.8 3.2 fusion.492
  205.0 2.6 fusion.493
  208.6 3.5 multiply_reduce_fusion.2
  215.0 3.2 fusion.492
  218.1 2.6 fusion.493
  221.8 3.5 multiply_reduce_fusion.2
  228.1 3.2 fusion.492
  231.3 2.6 fusion.493
  234.9 3.5 multiply_reduce_fusion.2
  241.2 3.2 fusion.492
  244.4 2.6 fusion.493
  248.1 3.5 multiply_reduce_fusion.2
  254.4 3.2 fusion.492
  257.5 2.6 fusion.493
  261.2 3.5 multiply_reduce_fusion.2
  267.5 3.2 fusion.492
  270.7 2.6 fusion.493
  275.0 5.9 %all-to-all-start.4 = ((f32[8,1,512]{2,1,0:T(1,128)}), f32[8,1,512]{2,1,0:T(1,128)S(1)}, u32[]{:S(2)}, u32[]{:S(2)}) async-start(f32[8,1,512]{2,1,0:T(1,128)} %reshape.21251), calls=%async_computation.4 | async-start | bytes 32768 | tf_op jit(solution)/shard_map/all_to_all | solution.py:206
  281.2 4.3 %scatter_fusion = f32[256,16,16]{2,1,0:T(8,128)S(1)} fusion(f32[256,16,16]{2,1,0:T(8,128)S(1)} %broadcast_in_dim.50, s32[128]{0:T(128)S(1)} %compare_select_fusion.5, f32[128,16,16]{2,1,0:T(8,128)S(1)} %bitcast.1797), kind=kCustom, calls=%fused_computation.10 | custom fusion | bytes 393728 | tf_op jit(solution)/shard_map/scatter | solution.py:189
  287.5 6.0 %all-to-all-start.5 = ((f32[8,1,8192]{2,1,0:T(1,128)}), f32[8,1,8192]{2,1,0:T(1,128)S(1)}, u32[]{:S(2)}, u32[]{:S(2)}) async-start(f32[8,1,8192]{2,1,0:T(1,128)} %reshape.21249), calls=%async_computation.5 | async-start | bytes 524288 | tf_op jit(solution)/shard_map/all_to_all | solution.py:205
  294.5 10.2 %psum.14 = f32[16,192]{1,0:T(8,128)S(1)} all-reduce(f32[16,192]{1,0:T(8,128)S(1)} %fusion.15), channel_id=1, replica_groups=mesh['zone'=8,'band'=4] {'band'}, use_global_device_ids=true, to_apply=%region_8.9 | all-reduce | flops 3072 | bytes 24576 | tf_op jit(solution)/shard_map/psum | solution.py:216
  308.4 33.8 %all-reduce.2.cloned.1.call-done = f32[16,16,192]{2,1,0:T(8,128)} async-done(((f32[16,16,192]{2,1,0:T(8,128)}), f32[16,16,192]{2,1,0:T(8,128)}) %all-reduce.2.cloned.1.call-update) | async-done | bytes 196624 | tf_op jit(solution)/shard_map/psum | solution.py:216
  358.5 6.1 %scatter_custom_fusion.4 = f32[3,640]{0,1:T(8,128)S(1)} fusion(s32[1024]{0:T(1024)S(1)} %bitcast.1984, f32[1024,3]{1,0:T(8,128)S(1)} %copy.183, f32[]{:T(128)} %constant.47.clone.1), kind=kCustom, calls=%fused_computation.56 | custom fusion | flops 3072 | bytes 7684 | tf_op jit(solution)/shard_map/scatter-add | solution.py:226
  364.6 3.4 collective-permute-start.2
  370.6 3.2 collective-permute-done.3
  (508 shorter events, 112.6 us)
Async XLA Ops:
  9.3 22.6 %all-to-all-start.1 = ((s32[8,1,32]{2,1,0:T(1,128)}), s32[8,1,32]{2,1,0:T(1,128)S(1)}, u32[]{:S(2)}, u32[]{:S(2)}) async-start(s32[8,1,32]{2,1,0:T(1,128)} %all_to_all.24), calls=%async_computation.1 | async-start | bytes 8192 | tf_op jit(solution)/shard_map/all_to_all | solution.py:176
  18.9 21.3 %collective-permute-start = (f32[2,64]{0,1:T(8,128)S(1)}, f32[2,64]{0,1:T(8,128)S(1)}, u32[]{:S(2)}, u32[]{:S(2)}) collective-permute-start(f32[2,64]{0,1:T(8,128)S(1)} %bitcast.1988), channel_id=1, source_target_pairs={{0,4},{4,8},{8,12},{12,16},{16,20},{20,24},{24,28},{1,5},{5,9},{9,... | collective-permute-start | bytes 1544 | tf_op jit(solution)/shard_map/ppermute | solution.py:19
  23.4 16.8 %collective-permute-start.1 = (f32[2,64]{0,1:T(8,128)S(1)}, f32[2,64]{0,1:T(8,128)S(1)}, u32[]{:S(2)}, u32[]{:S(2)}) collective-permute-start(f32[2,64]{0,1:T(8,128)S(1)} %bitcast.1989), channel_id=1, source_target_pairs={{4,0},{8,4},{12,8},{16,12},{20,16},{24,20},{28,24},{5,1},{9,5},{13... | collective-permute-start | bytes 1544 | tf_op jit(solution)/shard_map/ppermute | solution.py:22
  33.5 13.2 %all-to-all-start.3 = ((f32[8,1,512]{2,1,0:T(1,128)}), f32[8,1,512]{2,1,0:T(1,128)S(1)}, u32[]{:S(2)}, u32[]{:S(2)}) async-start(f32[8,1,512]{2,1,0:T(1,128)} %reshape.21247), calls=%async_computation.3 | async-start | bytes 32768 | tf_op jit(solution)/shard_map/all_to_all | solution.py:180
  46.7 11.3 %all-to-all-start.2 = ((f32[8,1,1024]{2,1,0:T(1,128)}), f32[8,1,1024]{2,1,0:T(1,128)S(1)}, u32[]{:S(2)}, u32[]{:S(2)}) async-start(f32[8,1,1024]{2,1,0:T(1,128)} %reshape.21245), calls=%async_computation.2 | async-start | bytes 65536 | tf_op jit(solution)/shard_map/all_to_all | solution.py:179
  58.0 217.0 %all-to-all-start = ((f32[8,32,2]{1,2,0:T(2,128)}), f32[8,32,2]{1,2,0:T(2,128)S(1)}, u32[]{:S(2)}, u32[]{:S(2)}) async-start(f32[8,32,2]{1,2,0:T(2,128)} %copy.177), calls=%async_computation | async-start | bytes 16384 | tf_op jit(solution)/shard_map/all_to_all | solution.py:207
  275.0 12.5 %all-to-all-start.4 = ((f32[8,1,512]{2,1,0:T(1,128)}), f32[8,1,512]{2,1,0:T(1,128)S(1)}, u32[]{:S(2)}, u32[]{:S(2)}) async-start(f32[8,1,512]{2,1,0:T(1,128)} %reshape.21251), calls=%async_computation.4 | async-start | bytes 32768 | tf_op jit(solution)/shard_map/all_to_all | solution.py:206
  287.5 17.3 %all-to-all-start.5 = ((f32[8,1,8192]{2,1,0:T(1,128)}), f32[8,1,8192]{2,1,0:T(1,128)S(1)}, u32[]{:S(2)}, u32[]{:S(2)}) async-start(f32[8,1,8192]{2,1,0:T(1,128)} %reshape.21249), calls=%async_computation.5 | async-start | bytes 524288 | tf_op jit(solution)/shard_map/all_to_all | solution.py:205
  293.5 48.7 %all-reduce.2.cloned.1.call-start = ((), (), s32[]{:S(2)}) async-start(), calls=%async_computation.6 | async-start | bytes 524288 | tf_op jit(solution)/shard_map/psum | solution.py:216
  342.2 13.9 %copy-start = (f32[16,16,192]{2,1,0:T(8,128)S(1)}, f32[16,16,192]{2,1,0:T(8,128)}, u32[]{:S(2)}) copy-start(f32[16,16,192]{2,1,0:T(8,128)} %all-reduce.2.cloned.1.call-done) | copy-start | bytes 589828
  364.6 5.0 %collective-permute-start.2 = (f32[3,64]{0,1:T(8,128)S(1)}, f32[3,64]{0,1:T(8,128)S(1)}, u32[]{:S(2)}, u32[]{:S(2)}) collective-permute-start(f32[3,64]{0,1:T(8,128)S(1)} %get-tuple-element.643), channel_id=1, source_target_pairs={{0,4},{4,8},{8,12},{12,16},{16,20},{20,24},{24,28},{1,5},{5,9},{9,... | collective-permute-start | bytes 2312 | tf_op jit(solution)/shard_map/ppermute | solution.py:19
  368.0 5.8 %collective-permute-start.3 = (f32[3,64]{0,1:T(8,128)S(1)}, f32[3,64]{0,1:T(8,128)S(1)}, u32[]{:S(2)}, u32[]{:S(2)}) collective-permute-start(f32[3,64]{0,1:T(8,128)S(1)} %get-tuple-element.642), channel_id=1, source_target_pairs={{4,0},{8,4},{12,8},{16,12},{20,16},{24,20},{28,24},{5,1},{9,5},{13... | collective-permute-start | bytes 2312 | tf_op jit(solution)/shard_map/ppermute | solution.py:22
Sparse Core Ops, SparseCore 0:
  308.5 33.6 all-reduce.1
where the time goes:
time: 385 us; the launch traced here: 382 us
  other arithmetic  98.7 us (26%)
  matrix products  93.2 us (24%)
  local copies, waits for them, and re-layouts  77.3 us (20%)
  starting transfers between devices  43.7 us (11%)
  waiting for transfers between devices  43.5 us (11%)
  between operations  13.9 us (4%)
  blocking collectives  10.2 us (3%)
    reduce_sum x16, other arithmetic, terms_per_tile(): jnp.sum(row_profile[:, :, :, None] * profile_col[:, :, None, :], axis=1)  55.8 us
    dot_general x16, matrix products, terms_per_tile(): normal = jnp.einsum('sp,tp->st', weighted, rendered, precision=HIGH)  50.5 us
    dot_general x16, matrix products, terms_per_tile(): jnp.einsum('sp,p->s', weighted, tile_image_pixels.reshape(-1), precision=...  41.3 us
    psum x1, waiting for transfers between devices, on_device(): matrices, vectors = lax.psum((matrices, vectors), 'band')  33.8 us
    reshape x16, local copies, waits for them, and re-layouts, terms_per_tile(): jnp.sum(row_profile[:, :, :, None] * profile_col[:, :, None, :], axis=1)  27.9 us
    dynamic_slice x112, local copies, waits for them, and re-layouts, stacked_terms(): lax.map(single_tile, (image_stack, pixel_weights, pixel_shifts, source_am...  17.8 us
    psum x1, blocking collectives, on_device(): matrices, vectors = lax.psum((matrices, vectors), 'band')  10.2 us
  transfers between devices with their start and end apart: 11, of which 5 were waited for; matrix products, arithmetic and copies ran while one was open for 62% of the time, Pallas kernels for 0%

commit v1 on v0

v1 whole, which is shorter than its diff:
```python
import functools

import jax
import jax.numpy as jnp
from jax import lax
from jax.experimental import pallas as pl
from jax.experimental.pallas import tpu as pltpu
from jax.sharding import PartitionSpec as P

FILTER_BANDS = 3
COMPS = 3
MAX_SOURCES = 16
LANES = 128
PACK = LANES // MAX_SOURCES
ROWS = 24
TILES_STEP = 4
PRIOR = 1.0

VMEM = pl.BlockSpec(memory_space=pltpu.VMEM)
SMEM = pl.BlockSpec(memory_space=pltpu.SMEM)


def exchange(block, moves, pick, slot, slots, sizes, ident):
    zones, bands = sizes
    piece = block.shape[-2:] if pick is None else block.shape[1:]

    def kernel(x_ref, o_ref, send_sem, recv_sem, own_sem):
        zone = lax.axis_index("zone")
        band = lax.axis_index("band")
        targets = [
            (lax.rem(zone + dz + zones, zones), lax.rem(band + db + bands, bands))
            for dz, db in moves
        ]
        barrier = pltpu.get_barrier_semaphore()
        for target in targets:
            pl.semaphore_signal(
                barrier, inc=1, device_id=target, device_id_type=pl.DeviceIdType.MESH
            )
        own_src = x_ref if pick is None else x_ref.at[pick(zone, band)]
        own = pltpu.make_async_copy(own_src, o_ref.at[slot(0, 0, zone, band)], own_sem)
        own.start()
        pl.semaphore_wait(barrier, len(moves))
        copies = []
        for order, ((dz, db), target) in enumerate(zip(moves, targets)):
            copy = pltpu.make_async_remote_copy(
                src_ref=x_ref if pick is None else x_ref.at[pick(*target)],
                dst_ref=o_ref.at[slot(dz, db, zone, band)],
                send_sem=send_sem.at[order],
                recv_sem=recv_sem.at[order],
                device_id=target,
                device_id_type=pl.DeviceIdType.MESH,
            )
            copy.start()
            copies.append(copy)
        own.wait()
        for copy in copies:
            copy.wait()

    return pl.pallas_call(
        kernel,
        out_shape=jax.ShapeDtypeStruct((slots,) + piece, block.dtype),
        in_specs=[VMEM],
        out_specs=VMEM,
        scratch_shapes=[
            pltpu.SemaphoreType.DMA((len(moves),)),
            pltpu.SemaphoreType.DMA((len(moves),)),
            pltpu.SemaphoreType.DMA,
        ],
        compiler_params=pltpu.CompilerParams(collective_id=ident, has_side_effects=True),
    )(block)


def lane_take(row, index):
    table = jnp.broadcast_to(row, index.shape)
    return jnp.take_along_axis(table, index, axis=1, mode="promise_in_bounds")


def lookup(rows, index):
    found = jnp.zeros(index.shape, rows[0].dtype)
    low = index & (LANES - 1)
    for part, row in enumerate(rows):
        found = jnp.where(index // LANES == part, lane_take(row, low), found)
    return found


class Catalog:
    def __init__(self, sources, edge, blobs):
        self.parts = sources // LANES
        self.edge_row = 2 * self.parts
        self.count_row = self.edge_row + 1
        self.member_row = -(-(self.count_row + 1) // 8) * 8
        self.member_rows = blobs // PACK
        self.rows = self.member_row + -(-self.member_rows // 8) * 8
        self.sources, self.edge, self.blobs = sources, edge, blobs

    def pack(self, source_pos, edge_rows, blob_members, counts):
        pieces = [
            source_pos.reshape(-1, LANES),
            edge_rows.astype(jnp.float32).reshape(1, LANES),
            jnp.pad(counts.astype(jnp.float32), (0, LANES - counts.shape[0])).reshape(1, LANES),
            jnp.zeros((self.member_row - self.count_row - 1, LANES), jnp.float32),
            blob_members.astype(jnp.float32).reshape(-1, LANES),
        ]
        return jnp.concatenate(pieces, axis=0)

    def members(self, ref, zone):
        return ref[zone, self.member_row : self.member_row + self.member_rows, :].astype(jnp.int32)

    def edges(self, ref, zone):
        return ref[zone, self.edge_row : self.edge_row + 1, :].astype(jnp.int32)

    def live(self, ref, zone):
        shape = (self.member_rows, LANES)
        lane = lax.broadcasted_iota(jnp.int32, shape, 1)
        row = lax.broadcasted_iota(jnp.int32, shape, 0)
        counts = ref[zone, self.count_row : self.count_row + 1, :].astype(jnp.int32)
        held = lane_take(counts, row * PACK + lane // MAX_SOURCES)
        return (lane % MAX_SOURCES) < held


def resolve(cat, zones, cat_ref, edge_ref, table_ref):
    def edge_body(zone, carry):
        index = jnp.broadcast_to(cat.edges(cat_ref, zone), (8, LANES))
        for coord in range(2):
            rows = [
                cat_ref[zone, coord * cat.parts + part : coord * cat.parts + part + 1, :]
                for part in range(cat.parts)
            ]
            edge_ref[coord, zone] = lookup(rows, index)
        return carry

    lax.fori_loop(0, zones, edge_body, 0)

    def member_body(zone, carry):
        member = cat.members(cat_ref, zone)
        before = jnp.maximum(zone - 1, 0)
        after = jnp.minimum(zone + 1, zones - 1)
        lane = lax.broadcasted_iota(jnp.int32, (8, LANES), 1)
        low = member < cat.edge
        high = member >= cat.edge + cat.sources
        own = jnp.clip(member - cat.edge, 0, cat.sources - 1)
        rim = jnp.where(low, cat.edge + member, jnp.where(high, member - cat.edge - cat.sources, 0))
        start = pl.multiple_of(zone * cat.member_rows, 8)
        for coord in range(2):
            rows = [
                cat_ref[zone, coord * cat.parts + part : coord * cat.parts + part + 1, :]
                for part in range(cat.parts)
            ]
            table = jnp.where(lane >= cat.edge, edge_ref[coord, before], edge_ref[coord, after])
            at_rim = lane_take(table[:1], rim)
            table_ref[coord, pl.ds(start, cat.member_rows), :] = jnp.where(
                low | high, at_rim, lookup(rows, own)
            )
        table_ref[2, pl.ds(start, cat.member_rows), :] = cat.live(cat_ref, zone).astype(jnp.float32)
        return carry

    lax.fori_loop(0, zones, member_body, 0)


def tile_kernel(
    cat, zones, groups,
    blob_ref, band_ref, shift_ref, amp_ref, spread_ref,
    cat_ref, pixel_ref, weight_ref,
    out_ref, edge_ref, table_ref, factor_ref, used_ref,
):
    step = pl.program_id(0)
    height = pixel_ref.shape[1]

    @pl.when(step == 0)
    def _():
        out_ref[...] = jnp.zeros_like(out_ref)
        for zone in range(zones):
            used_ref[zone] = 0
        resolve(cat, zones, cat_ref, edge_ref, table_ref)

    shape = (MAX_SOURCES, LANES)
    lane = lax.broadcasted_iota(jnp.int32, shape, 1)
    sub = lax.broadcasted_iota(jnp.int32, shape, 0)
    lane_f = lane.astype(jnp.float32)
    row_f = (lane % height).astype(jnp.float32)
    comp = lane // height
    upper = sub < 8

    for slot in range(pixel_ref.shape[0]):
        tile = step * pixel_ref.shape[0] + slot
        blob = blob_ref[tile]
        at = blob // PACK
        mine = lane == (blob % PACK) * MAX_SOURCES + sub
        row_pos, col_pos, live = [
            jnp.sum(
                jnp.where(mine, jnp.broadcast_to(table_ref[k, pl.ds(at, 1), :], shape), 0.0),
                axis=1,
                keepdims=True,
            )
            for k in range(3)
        ]
        spread = [spread_ref[g, tile] for g in range(COMPS)]
        amp = [amp_ref[g, tile] for g in range(COMPS)]
        row_spread = jnp.where(comp == 0, spread[0], jnp.where(comp == 1, spread[1], spread[2]))
        row_amp = jnp.where(comp == 0, amp[0], jnp.where(comp == 1, amp[1], amp[2]))
        drow = row_f - shift_ref[0, tile] - row_pos
        rows = jnp.exp(-row_spread * (drow * drow)) * (row_amp * live)
        dcol = lane_f - shift_ref[1, tile] - col_pos
        dcol = dcol * dcol
        cols = [jnp.exp(-spread[g] * dcol) for g in range(COMPS)]
        root = jnp.sqrt(weight_ref[slot])
        image = root * pixel_ref[slot]
        for i in range(height):
            model = rows[:, i : i + 1] * cols[0]
            for g in range(1, COMPS):
                model = model + rows[:, g * height + i : g * height + i + 1] * cols[g]
            scaled = model * root[i : i + 1, :]
            head = scaled.astype(jnp.bfloat16)
            tail = (scaled - head.astype(jnp.float32)).astype(jnp.bfloat16)
            line = jnp.broadcast_to(image[i : i + 1, :], shape)
            line_head = line.astype(jnp.bfloat16).astype(jnp.float32)
            seen = jnp.where(upper, line_head, line - line_head).astype(jnp.bfloat16)
            where = slice(i * LANES, (i + 1) * LANES)
            factor_ref[slot, 0:16, where] = head
            factor_ref[slot, 16:32, where] = tail
            factor_ref[slot, 32:48, where] = seen
        product = lax.dot_general(
            factor_ref[slot],
            factor_ref[slot, 0:32, :],
            (((1,), (1,)), ((), ())),
            preferred_element_type=jnp.float32,
        )
        folded = product[:, :16] + product[:, 16:]
        normal = folded[:16] + folded[16:32]
        vector = folded[32:40] + folded[40:48]
        zone = blob // cat.blobs
        code = band_ref[tile] * cat.blobs + blob % cat.blobs
        eight = lax.broadcasted_iota(jnp.int32, vector.shape, 0)
        tailrows = jnp.where(
            eight == 0, vector, jnp.where(eight == 1, code.astype(jnp.float32), 0.0)
        )
        entry = jnp.concatenate([normal, tailrows], axis=0)
        entry = jnp.concatenate(
            [entry, jnp.zeros((ROWS, LANES - MAX_SOURCES), jnp.float32)], axis=1
        )
        order = used_ref[zone]
        used_ref[zone] = order + 1
        seat = order % PACK
        entry = pltpu.roll(entry, seat * MAX_SOURCES, 1)
        place = zone * groups + order // PACK
        out_ref[place] = out_ref[place] + entry


def tile_terms(cat, zones, groups, blob, band, shift, amp, spread, catalogs, pixels, weights):
    tiles, height, width = pixels.shape
    per = TILES_STEP
    while tiles % per:
        per -= 1
    block = pl.BlockSpec((per, height, width), lambda s: (s, 0, 0))
    return pl.pallas_call(
        functools.partial(tile_kernel, cat, zones, groups),
        grid=(tiles // per,),
        out_shape=jax.ShapeDtypeStruct((zones * groups, ROWS, LANES), jnp.float32),
        in_specs=[SMEM] * 5 + [VMEM, block, block],
        out_specs=pl.BlockSpec((zones * groups, ROWS, LANES), lambda s: (0, 0, 0)),
        scratch_shapes=[
            pltpu.VMEM((2, zones, 8, LANES), jnp.float32),
            pltpu.VMEM((3, zones * cat.member_rows, LANES), jnp.float32),
            pltpu.VMEM((per, 48, height * width), jnp.bfloat16),
            pltpu.SMEM((zones,), jnp.int32),
        ],
        compiler_params=pltpu.CompilerParams(dimension_semantics=("arbitrary",)),
    )(blob, band, shift, amp, spread, catalogs, pixels, weights)


def gather_kernel(capacity, groups, code_ref, got_ref, total_ref):
    total_ref[...] = jnp.zeros_like(total_ref)
    lane = lax.broadcasted_iota(jnp.int32, (ROWS, LANES), 1) // MAX_SOURCES

    def body(group, carry):
        block = got_ref[group]
        for seat in range(min(PACK, capacity)):
            code = code_ref[group, seat]
            to = code % PACK
            moved = pltpu.roll(block, ((to - seat + PACK) % PACK) * MAX_SOURCES, 1)
            place = code // PACK
            total_ref[place] = total_ref[place] + jnp.where(lane == to, moved, 0.0)
        return carry

    lax.fori_loop(0, got_ref.shape[0], body, 0)


def solve_kernel(got_ref, out_ref):
    total = got_ref[0]
    for other in range(1, got_ref.shape[0]):
        total = total + got_ref[other]
    for group in range(total.shape[0]):
        block = total[group]
        row = lax.broadcasted_iota(jnp.int32, (ROWS, LANES), 0)
        lane = lax.broadcasted_iota(jnp.int32, (ROWS, LANES), 1)
        column = lane % MAX_SOURCES
        first = lane - column
        block = block + jnp.where(row == column, PRIOR, 0.0)
        scale = jnp.ones((1, LANES), jnp.float32)
        for k in range(MAX_SOURCES):
            taken = jnp.take_along_axis(block, first + k, axis=1, mode="promise_in_bounds")
            pivot = taken[k : k + 1]
            across = block[k : k + 1]
            scale = jnp.where(column[:1] == k, across, scale)
            ratio = jnp.where(column[:1] == k, 0.0, across / pivot)
            block = block - taken * ratio
        out_ref[group : group + 1, :] = block[MAX_SOURCES : MAX_SOURCES + 1] / scale
    out_ref[total.shape[0] :, :] = jnp.zeros(
        (out_ref.shape[0] - total.shape[0], LANES), jnp.float32
    )


def place_kernel(cat, zones, bands, share, zone_ref, cat_ref, flux_ref, out_ref, pick_ref):
    zone = zone_ref[0]
    edges = cat.edges(cat_ref, zone)
    rows = cat.member_rows
    total = jnp.zeros((16, cat.sources), jnp.float32)
    source = lax.broadcasted_iota(jnp.int32, (cat.sources, LANES), 0)
    for side in range(3):
        near = jnp.clip(zone + side - 1, 0, zones - 1)
        member = cat.members(cat_ref, near)
        live = cat.live(cat_ref, near)
        if side == 0:
            valid = (member >= cat.edge + cat.sources) & (zone > 0)
            target = lane_take(edges, jnp.where(valid, member - cat.edge - cat.sources, 0))
        elif side == 1:
            valid = (member >= cat.edge) & (member < cat.edge + cat.sources)
            target = member - cat.edge
        else:
            valid = (member < cat.edge) & (zone < zones - 1)
            target = lane_take(edges, jnp.where(valid, member + cat.edge, 0))
        valid = valid & live
        target = jnp.where(valid, target, -1)
        parts = []
        for band in range(FILTER_BANDS):
            lines = []
            for row in range(rows):
                group = band * rows + row
                lines.append(flux_ref[side * bands + group // share, group % share : group % share + 1, :])
            parts.append(jnp.concatenate(lines, axis=1))
        values = jnp.concatenate(parts, axis=0)
        pieces = []
        for _ in range(3):
            piece = values.astype(jnp.bfloat16).astype(jnp.float32)
            values = values - piece
            pieces.append(piece)
        pieces.append(jnp.zeros((16 - 3 * FILTER_BANDS, values.shape[1]), jnp.float32))
        left = jnp.concatenate(pieces, axis=0).astype(jnp.bfloat16)
        for row in range(rows):
            hit = source == target[row : row + 1, :]
            pick_ref[:, row * LANES : (row + 1) * LANES] = jnp.where(hit, 1.0, 0.0).astype(jnp.bfloat16)
        total = total + lax.dot_general(
            left, pick_ref[...], (((1,), (1,)), ((), ())), preferred_element_type=jnp.float32
        )
    out_ref[...] = total[0:3] + total[3:6] + total[6:9]


def on_device(
    sizes, pixels, inv_var, tile_offset, psf_amp, psf_sigma, tile_blob, tile_band,
    source_pos, edge_rows, blob_members, sources_per_blob,
):
    zones, bands = sizes
    blobs = sources_per_blob.shape[0]
    sources = source_pos.shape[1]
    tiles = pixels.shape[0]
    cat = Catalog(sources, edge_rows.shape[0] // 2, blobs)
    capacity = max(2, (2 * tiles + zones - 1) // zones)
    groups = -(-capacity // PACK)
    systems = FILTER_BANDS * blobs // PACK
    share = systems // bands
    zone_moves = [(d, 0) for d in range(1, zones)]
    band_moves = [(0, d) for d in range(1, bands)]
    near_moves = [(dz, db) for dz in (-1, 0, 1) for db in range(bands) if dz or db]

    packed = cat.pack(source_pos, edge_rows, blob_members, sources_per_blob)
    catalogs = exchange(packed, zone_moves, None, lambda dz, db, z, b: z, zones, sizes, 0)
    spread = 0.5 / (psf_sigma * psf_sigma)
    terms = tile_terms(
        cat, zones, groups, tile_blob, tile_band, tile_offset, psf_amp, spread, catalogs,
        pixels, inv_var,
    )
    got = exchange(
        terms.reshape(zones, groups * ROWS, LANES),
        zone_moves, lambda z, b: z, lambda dz, db, z, b: z, zones, sizes, 1,
    ).reshape(zones * groups, ROWS, LANES)
    codes = got[:, MAX_SOURCES + 1, ::MAX_SOURCES].astype(jnp.int32)
    totals = pl.pallas_call(
        functools.partial(gather_kernel, capacity, groups),
        out_shape=jax.ShapeDtypeStruct((systems, ROWS, LANES), jnp.float32),
        in_specs=[SMEM, VMEM],
        out_specs=VMEM,
    )(codes, got)
    shares = exchange(
        totals.reshape(bands, share * ROWS, LANES),
        band_moves, lambda z, b: b, lambda dz, db, z, b: b, bands, sizes, 2,
    )
    solved = pl.pallas_call(
        solve_kernel,
        out_shape=jax.ShapeDtypeStruct((-(-share // 8) * 8, LANES), jnp.float32),
        in_specs=[VMEM],
        out_specs=VMEM,
    )(shares.reshape(bands, share, ROWS, LANES))
    fluxes = exchange(
        solved, near_moves, None, lambda dz, db, z, b: (1 - dz) * bands + b, 3 * bands, sizes, 3
    )
    return pl.pallas_call(
        functools.partial(place_kernel, cat, zones, bands, share),
        out_shape=jax.ShapeDtypeStruct((FILTER_BANDS, sources), jnp.float32),
        in_specs=[SMEM, VMEM, VMEM],
        out_specs=VMEM,
        scratch_shapes=[pltpu.VMEM((sources, cat.member_rows * LANES), jnp.bfloat16)],
    )(lax.axis_index("zone").reshape(1), catalogs, fluxes)


def solution(mesh):
    sizes = (mesh.shape["zone"], mesh.shape["band"])
    return jax.shard_map(
        functools.partial(on_device, sizes),
        mesh=mesh,
        in_specs=(
            P(("zone", "band"), None, None),
            P(("zone", "band"), None, None),
            P(None, ("zone", "band")),
            P(None, ("zone", "band")),
            P(None, ("zone", "band")),
            P(("zone", "band")),
            P(("zone", "band")),
            P(None, "zone"),
            P("zone"),
            P("zone", None),
            P("zone"),
        ),
        out_specs=P(None, "zone"),
        check_vma=False,
    )
```

time: 385 us -> 152 us (0.39)
  Pallas kernels: 0 us -> 143 us
  other arithmetic: 98.7 us -> 3.89 us
  matrix products: 93.2 us -> 0 us
  local copies, waits for them, and re-layouts: 77.3 us -> 3.72 us
  starting transfers between devices: 43.7 us -> 0 us
  waiting for transfers between devices: 43.5 us -> 0 us
  between operations: 13.9 us -> 0.05 us
  blocking collectives: 10.2 us -> 0 us
    pallas_call x0 -> x8, Pallas kernels: none -> 143 us  [the longest x1 91.4 us: tile_terms(): pl.pallas_call(functools.partial(tile_kernel, cat, zones, groups), grid=(...]
    dot_general x34 -> x0, matrix products: 93.2 us -> none  [the longest x16 50.5 us: terms_per_tile(): normal = jnp.einsum('sp,tp->st', weighted, rendered, precision=HIGH)]
    reduce_sum x17 -> x0, other arithmetic: 56 us -> none  [the longest x16 55.8 us: terms_per_tile(): jnp.sum(row_profile[:, :, :, None] * profile_col[:, :, None, :], axis=1)]
    psum x1 -> x0, waiting for transfers between devices: 33.8 us -> none  [on_device(): matrices, vectors = lax.psum((matrices, vectors), 'band')]
    all_to_all x6 -> x0, starting transfers between devices: 33.8 us -> none  [the longest x1 7.31 us: on_device(): lax.all_to_all(asked, 'zone', split_axis=0, concat_axis=0, tiled=True)]
    reshape x28 -> x3, local copies, waits for them, and re-layouts: 32.4 us -> 0.78 us  [the longest x1 0.7 us: pack(): source_pos.reshape(-1, LANES)]
    dynamic_slice x112 -> x0, local copies, waits for them, and re-layouts: 17.8 us -> none  [stacked_terms(): lax.map(single_tile, (image_stack, pixel_weights, pixel_shifts, source_am...]
    psum x1 -> x0, blocking collectives: 10.2 us -> none  [on_device(): matrices, vectors = lax.psum((matrices, vectors), 'band')]
  transfers between devices with their start and end apart: 11 -> 0, of which waited for: 5 -> 0; matrix products, arithmetic and copies ran while one was open for 62% -> 0% of each run, Pallas kernels for 0% -> 0%
where the time goes in v1:
time: 152 us; the launch traced here: 151 us
  Pallas kernels  143 us (94%)
  other arithmetic  3.89 us (3%)
  local copies, waits for them, and re-layouts  3.72 us (2%)
    pallas_call x1, Pallas kernels, tile_terms(): pl.pallas_call(functools.partial(tile_kernel, cat, zones, groups), grid=(...  91.4 us
    pallas_call x4, Pallas kernels, exchange(): pl.pallas_call(kernel, out_shape=jax.ShapeDtypeStruct((slots,) + piece, b...  40.2 us
    pallas_call x1, Pallas kernels, on_device(): pl.pallas_call(functools.partial(gather_kernel, capacity, groups), out_sh...  5.63 us
    pallas_call x1, Pallas kernels, on_device(): pl.pallas_call(functools.partial(place_kernel, cat, zones, bands, share),...  3.35 us

profile of v1, /device:TPU:0, one launch (start us, length us, event | category | flops | bytes accessed | tf_op | source)
XLA Modules:
  0.0 151.1 jit_solution(4859316916553863369)
XLA Ops:
  0.0 0.7 convert_element_type.18
  0.7 0.1 copy.13
  0.8 0.1 reshape.32
  0.9 0.7 reshape.29
  1.6 0.7 convert_element_type.17
  2.2 0.7 convert_bitcast_fusion
  2.9 1.8 %concatenate.3.x_ref = f32[24,128]{1,0:T(8,128)} concatenate(f32[8,128]{1,0:T(8,128)S(1)} %reshape.29, f32[1,128]{1,0:T(1,128)S(1)} %convert_bitcast_fusion, f32[1,128]{1,0:T(1,128)S(1)} %pad_bitcast_fusion, f32[6,128]{1,0:T(8,128)S(1)} %broadcast_in_dim.3, f32[8,128]{1,0:T(8,128)S(1)} %reshape.32), dimensions={0} | concatenate | bytes 24576 | tf_op jit(solution)/shard_map/concatenate | solution.py:104
  4.7 10.3 %shard_map.109.cat_ref = f32[8,24,128]{2,1,0:T(8,128)} custom-call(f32[24,128]{1,0:T(8,128)} %concatenate.3.x_ref), custom_call_target="tpu_custom_call" | custom-call | tf_op jit(solution)/shard_map/pallas_call | solution.py:59
  15.0 1.3 multiply_divide_fusion.spread_ref
  16.2 91.4 %shard_map.110 = f32[32,24,128]{2,1,0:T(8,128)} custom-call(s32[128]{0:T(128)} %blob_ref.1, s32[128]{0:T(128)} %band_ref.1, f32[2,128]{1,0:T(2,128)} %shift_ref.1, f32[3,128]{1,0:T(4,128)} %amp_ref.1, f32[3,128]{1,0:T(4,128)} %multiply_divide_fusion.spread_ref, f32[8,24,128]{2,1,0:T(8,128)} %shard_map.109.cat_ref, f32[128,32,128]{2,1,0:T(8,128)} %pixel_ref.1, ...), custom_call_target="tpu_custom_call" | custom-call | tf_op jit(solution)/shard_map/pallas_call | solution.py:255
  107.6 11.6 %shard_map.111 = f32[8,96,128]{2,1,0:T(8,128)} custom-call(f32[8,96,128]{2,1,0:T(8,128)} %bitcast.12), custom_call_target="tpu_custom_call" | custom-call | tf_op jit(solution)/shard_map/pallas_call | solution.py:59
  119.2 1.1 slice.3
  120.3 0.6 convert_element_type.19
  120.9 5.6 %shard_map.112 = f32[24,24,128]{2,1,0:T(8,128)} custom-call(s32[32,8]{1,0:T(8,128)} %bitcast.15, f32[32,24,128]{2,1,0:T(8,128)} %bitcast.11), custom_call_target="tpu_custom_call" | custom-call | tf_op jit(solution)/shard_map/pallas_call | solution.py:387
  126.5 6.9 %shard_map.113 = f32[4,144,128]{2,1,0:T(8,128)} custom-call(f32[4,144,128]{2,1,0:T(8,128)} %bitcast.14), custom_call_target="tpu_custom_call" | custom-call | tf_op jit(solution)/shard_map/pallas_call | solution.py:59
  133.4 2.9 %shard_map.114.x_ref = f32[8,128]{1,0:T(8,128)} custom-call(f32[4,6,24,128]{3,2,1,0:T(8,128)} %bitcast.13), custom_call_target="tpu_custom_call" | custom-call | tf_op jit(solution)/shard_map/pallas_call | solution.py:397
  136.3 11.5 %shard_map.115.flux_ref = f32[12,8,128]{2,1,0:T(8,128)} custom-call(f32[8,128]{1,0:T(8,128)} %shard_map.114.x_ref), custom_call_target="tpu_custom_call" | custom-call | tf_op jit(solution)/shard_map/pallas_call | solution.py:59
  147.8 3.3 %shard_map.116 = f32[3,512]{1,0:T(4,128)} custom-call(s32[1]{0:T(128)} %bitcast.zone_ref, f32[8,24,128]{2,1,0:T(8,128)} %shard_map.109.cat_ref, f32[12,8,128]{2,1,0:T(8,128)} %shard_map.115.flux_ref), custom_call_target="tpu_custom_call" | custom-call | tf_op jit(solution)/shard_map/pallas_call | solution.py:406
  (2 shorter events, 0.0 us)

commit v2 on v1

--- a/solution.py
+++ b/solution.py
@@ -161,7 +161,7 @@
     cat, zones, groups,
     blob_ref, band_ref, shift_ref, amp_ref, spread_ref,
     cat_ref, pixel_ref, weight_ref,
-    out_ref, edge_ref, table_ref, factor_ref, used_ref,
+    out_ref, edge_ref, table_ref, factor_ref, line_ref, used_ref,
 ):
     step = pl.program_id(0)
     height = pixel_ref.shape[1]
@@ -173,48 +173,93 @@
             used_ref[zone] = 0
         resolve(cat, zones, cat_ref, edge_ref, table_ref)
 
+    half = MAX_SOURCES // 2
     shape = (MAX_SOURCES, LANES)
     lane = lax.broadcasted_iota(jnp.int32, shape, 1)
     sub = lax.broadcasted_iota(jnp.int32, shape, 0)
     lane_f = lane.astype(jnp.float32)
-    row_f = (lane % height).astype(jnp.float32)
-    comp = lane // height
-    upper = sub < 8
+    keep = (lane % half) == (sub % half)
+    tall = (height, LANES)
+    tall_lane = lax.broadcasted_iota(jnp.int32, tall, 1)
+    row_f = lax.broadcasted_iota(jnp.int32, tall, 0).astype(jnp.float32)
+    eight_lane = tall_lane[:8]
+    comp = (eight_lane[:1] // half) % COMPS
+    width = COMPS * half
+    high_part = (tall_lane < width) | (tall_lane >= 2 * width)
+    used_part = tall_lane < 3 * width
+    blank = jnp.zeros((LANES - 3 * width, LANES), jnp.float32)
 
     for slot in range(pixel_ref.shape[0]):
         tile = step * pixel_ref.shape[0] + slot
         blob = blob_ref[tile]
         at = blob // PACK
-        mine = lane == (blob % PACK) * MAX_SOURCES + sub
-        row_pos, col_pos, live = [
-            jnp.sum(
-                jnp.where(mine, jnp.broadcast_to(table_ref[k, pl.ds(at, 1), :], shape), 0.0),
-                axis=1,
-                keepdims=True,
-            )
-            for k in range(3)
+        offset = (blob % PACK) * MAX_SOURCES
+        table = [
+            jnp.broadcast_to(table_ref[k, pl.ds(at, 1), :], shape) for k in range(3)
         ]
+        col_pos = jnp.sum(
+            jnp.where(lane == offset + sub, table[1], 0.0), axis=1, keepdims=True
+        )
         spread = [spread_ref[g, tile] for g in range(COMPS)]
         amp = [amp_ref[g, tile] for g in range(COMPS)]
         row_spread = jnp.where(comp == 0, spread[0], jnp.where(comp == 1, spread[1], spread[2]))
         row_amp = jnp.where(comp == 0, amp[0], jnp.where(comp == 1, amp[1], amp[2]))
-        drow = row_f - shift_ref[0, tile] - row_pos
-        rows = jnp.exp(-row_spread * (drow * drow)) * (row_amp * live)
         dcol = lane_f - shift_ref[1, tile] - col_pos
         dcol = dcol * dcol
         cols = [jnp.exp(-spread[g] * dcol) for g in range(COMPS)]
+        cols_head = [col.astype(jnp.bfloat16).astype(jnp.float32) for col in cols]
+        cols_tail = [col - head for col, head in zip(cols, cols_head)]
         root = jnp.sqrt(weight_ref[slot])
         image = root * pixel_ref[slot]
+        image_head = image.astype(jnp.bfloat16).astype(jnp.float32)
+        line_ref[slot, 0] = root
+        line_ref[slot, 1] = image_head
+        line_ref[slot, 2] = image - image_head
+        models = []
+        for h in range(2):
+            index = offset + h * half + eight_lane % half
+            row_pos = jnp.take_along_axis(table[0][:8], index, axis=1, mode="promise_in_bounds")
+            live = jnp.take_along_axis(table[2][:8], index, axis=1, mode="promise_in_bounds")
+            drow = row_f - shift_ref[0, tile] - row_pos[:1]
+            rows = jnp.exp(-row_spread * (drow * drow)) * (row_amp * live[:1])
+            rows_head = rows.astype(jnp.bfloat16).astype(jnp.float32)
+            line_ref[slot, 3 + h] = jnp.where(
+                used_part, jnp.where(high_part, rows_head, rows - rows_head), 0.0
+            )
+            span = slice(h * half, (h + 1) * half)
+            heads = [c[span] for c in cols_head]
+            right = jnp.concatenate(
+                heads + heads + [c[span] for c in cols_tail] + [blank], axis=0
+            ).astype(jnp.bfloat16)
+            left = []
+            for i in range(0, height, 2):
+                pair = jnp.concatenate(
+                    [
+                        jnp.broadcast_to(line_ref[slot, 3 + h, i + d : i + d + 1, :], (half, LANES))
+                        for d in range(2)
+                    ],
+                    axis=0,
+                )
+                left.append(jnp.where(keep, pair, 0.0).astype(jnp.bfloat16))
+            models.append(
+                lax.dot_general(
+                    jnp.concatenate(left, axis=0), right, (((1,), (0,)), ((), ())),
+                    preferred_element_type=jnp.float32,
+                )
+            )
         for i in range(height):
-            model = rows[:, i : i + 1] * cols[0]
-            for g in range(1, COMPS):
-                model = model + rows[:, g * height + i : g * height + i + 1] * cols[g]
-            scaled = model * root[i : i + 1, :]
+            span = slice(i * half, (i + 1) * half)
+            weight = jnp.broadcast_to(line_ref[slot, 0, i : i + 1, :], shape)
+            scaled = jnp.concatenate([models[0][span], models[1][span]], axis=0) * weight
             head = scaled.astype(jnp.bfloat16)
             tail = (scaled - head.astype(jnp.float32)).astype(jnp.bfloat16)
-            line = jnp.broadcast_to(image[i : i + 1, :], shape)
-            line_head = line.astype(jnp.bfloat16).astype(jnp.float32)
-            seen = jnp.where(upper, line_head, line - line_head).astype(jnp.bfloat16)
+            seen = jnp.concatenate(
+                [
+                    jnp.broadcast_to(line_ref[slot, k, i : i + 1, :], (half, LANES))
+                    for k in (1, 2)
+                ],
+                axis=0,
+            ).astype(jnp.bfloat16)
             where = slice(i * LANES, (i + 1) * LANES)
             factor_ref[slot, 0:16, where] = head
             factor_ref[slot, 16:32, where] = tail
@@ -262,6 +307,7 @@
             pltpu.VMEM((2, zones, 8, LANES), jnp.float32),
             pltpu.VMEM((3, zones * cat.member_rows, LANES), jnp.float32),
             pltpu.VMEM((per, 48, height * width), jnp.bfloat16),
+            pltpu.VMEM((per, 5, height, width), jnp.float32),
             pltpu.SMEM((zones,), jnp.int32),
         ],
         compiler_params=pltpu.CompilerParams(dimension_semantics=("arbitrary",)),
@@ -285,39 +331,59 @@
     lax.fori_loop(0, got_ref.shape[0], body, 0)
 
 
-def solve_kernel(got_ref, out_ref):
-    total = got_ref[0]
-    for other in range(1, got_ref.shape[0]):
-        total = total + got_ref[other]
-    for group in range(total.shape[0]):
-        block = total[group]
-        row = lax.broadcasted_iota(jnp.int32, (ROWS, LANES), 0)
-        lane = lax.broadcasted_iota(jnp.int32, (ROWS, LANES), 1)
-        column = lane % MAX_SOURCES
-        first = lane - column
-        block = block + jnp.where(row == column, PRIOR, 0.0)
-        scale = jnp.ones((1, LANES), jnp.float32)
-        for k in range(MAX_SOURCES):
-            taken = jnp.take_along_axis(block, first + k, axis=1, mode="promise_in_bounds")
-            pivot = taken[k : k + 1]
-            across = block[k : k + 1]
-            scale = jnp.where(column[:1] == k, across, scale)
-            ratio = jnp.where(column[:1] == k, 0.0, across / pivot)
-            block = block - taken * ratio
-        out_ref[group : group + 1, :] = block[MAX_SOURCES : MAX_SOURCES + 1] / scale
-    out_ref[total.shape[0] :, :] = jnp.zeros(
-        (out_ref.shape[0] - total.shape[0], LANES), jnp.float32
-    )
-
-
-def place_kernel(cat, zones, bands, share, zone_ref, cat_ref, flux_ref, out_ref, pick_ref):
-    zone = zone_ref[0]
+def solve_group(block):
+    row = lax.broadcasted_iota(jnp.int32, (ROWS, LANES), 0)
+    lane = lax.broadcasted_iota(jnp.int32, (ROWS, LANES), 1)
+    column = lane % MAX_SOURCES
+    first = lane - column
+    block = block + jnp.where(row == column, PRIOR, 0.0)
+    scale = jnp.ones((1, LANES), jnp.float32)
+    for k in range(MAX_SOURCES):
+        taken = jnp.take_along_axis(block, first + k, axis=1, mode="promise_in_bounds")
+        pivot = taken[k : k + 1]
+        across = block[k : k + 1]
+        scale = jnp.where(column[:1] == k, across, scale)
+        ratio = jnp.where(column[:1] == k, 0.0, across / pivot)
+        block = block - taken * ratio
+    return block[MAX_SOURCES : MAX_SOURCES + 1] / scale
+
+
+def finish_kernel(
+    cat, zones, bands, share, total_ref, cat_ref, out_ref,
+    got_ref, solved_ref, flux_ref, pick_ref,
+    send_sum, recv_sum, own_sum, send_flux, recv_flux, own_flux,
+):
+    zone = lax.axis_index("zone")
+    band = lax.axis_index("band")
+    moves = [(dz, db) for dz in (0, 1, -1) for db in range(bands) if dz or db]
+    targets = [
+        (lax.rem(zone + dz + zones, zones), lax.rem(band + db, bands)) for dz, db in moves
+    ]
+    barrier = pltpu.get_barrier_semaphore()
+    for target in targets:
+        pl.semaphore_signal(barrier, inc=1, device_id=target, device_id_type=pl.DeviceIdType.MESH)
+    own = pltpu.make_async_copy(total_ref.at[band], got_ref.at[band], own_sum)
+    own.start()
+    pl.semaphore_wait(barrier, len(moves))
+    sums = []
+    for order in range(bands - 1):
+        target = targets[order]
+        copy = pltpu.make_async_remote_copy(
+            src_ref=total_ref.at[target[1]],
+            dst_ref=got_ref.at[band],
+            send_sem=send_sum.at[order],
+            recv_sem=recv_sum.at[order],
+            device_id=target,
+            device_id_type=pl.DeviceIdType.MESH,
+        )
+        copy.start()
+        sums.append(copy)
+
     edges = cat.edges(cat_ref, zone)
     rows = cat.member_rows
-    total = jnp.zeros((16, cat.sources), jnp.float32)
     source = lax.broadcasted_iota(jnp.int32, (cat.sources, LANES), 0)
     for side in range(3):
-        near = jnp.clip(zone + side - 1, 0, zones - 1)
+        near = lax.rem(zone + side - 1 + zones, zones)
         member = cat.members(cat_ref, near)
         live = cat.live(cat_ref, near)
         if side == 0:
@@ -329,14 +395,52 @@
         else:
             valid = (member < cat.edge) & (zone < zones - 1)
             target = lane_take(edges, jnp.where(valid, member + cat.edge, 0))
-        valid = valid & live
-        target = jnp.where(valid, target, -1)
+        target = jnp.where(valid & live, target, -1)
+        for row in range(rows):
+            hit = source == target[row : row + 1, :]
+            pick_ref[side, :, row * LANES : (row + 1) * LANES] = jnp.where(hit, 1.0, 0.0).astype(
+                jnp.bfloat16
+            )
+
+    own.wait()
+    for copy in sums:
+        copy.wait()
+    for group in range(share):
+        span = slice(group * ROWS, (group + 1) * ROWS)
+        block = got_ref[0, span, :]
+        for other in range(1, bands):
+            block = block + got_ref[other, span, :]
+        solved_ref[group : group + 1, :] = solve_group(block)
+    if solved_ref.shape[0] > share:
+        solved_ref[share:, :] = jnp.zeros((solved_ref.shape[0] - share, LANES), jnp.float32)
+
+    own = pltpu.make_async_copy(solved_ref, flux_ref.at[bands + band], own_flux)
+    own.start()
+    copies = []
+    for order, ((dz, db), target) in enumerate(zip(moves, targets)):
+        copy = pltpu.make_async_remote_copy(
+            src_ref=solved_ref,
+            dst_ref=flux_ref.at[(1 - dz) * bands + band],
+            send_sem=send_flux.at[order],
+            recv_sem=recv_flux.at[order],
+            device_id=target,
+            device_id_type=pl.DeviceIdType.MESH,
+        )
+        copy.start()
+        copies.append(copy)
+    own.wait()
+    for copy in copies:
+        copy.wait()
+
+    total = jnp.zeros((16, cat.sources), jnp.float32)
+    for side in range(3):
         parts = []
-        for band in range(FILTER_BANDS):
+        for band_row in range(FILTER_BANDS):
             lines = []
             for row in range(rows):
-                group = band * rows + row
-                lines.append(flux_ref[side * bands + group // share, group % share : group % share + 1, :])
+                group = band_row * rows + row
+                at = group % share
+                lines.append(flux_ref[side * bands + group // share, at : at + 1, :])
             parts.append(jnp.concatenate(lines, axis=1))
         values = jnp.concatenate(parts, axis=0)
         pieces = []
@@ -346,11 +450,8 @@
             pieces.append(piece)
         pieces.append(jnp.zeros((16 - 3 * FILTER_BANDS, values.shape[1]), jnp.float32))
         left = jnp.concatenate(pieces, axis=0).astype(jnp.bfloat16)
-        for row in range(rows):
-            hit = source == target[row : row + 1, :]
-            pick_ref[:, row * LANES : (row + 1) * LANES] = jnp.where(hit, 1.0, 0.0).astype(jnp.bfloat16)
         total = total + lax.dot_general(
-            left, pick_ref[...], (((1,), (1,)), ((), ())), preferred_element_type=jnp.float32
+            left, pick_ref[side], (((1,), (1,)), ((), ())), preferred_element_type=jnp.float32
         )
     out_ref[...] = total[0:3] + total[3:6] + total[6:9]
 
@@ -369,8 +470,6 @@
     systems = FILTER_BANDS * blobs // PACK
     share = systems // bands
     zone_moves = [(d, 0) for d in range(1, zones)]
-    band_moves = [(0, d) for d in range(1, bands)]
-    near_moves = [(dz, db) for dz in (-1, 0, 1) for db in range(bands) if dz or db]
 
     packed = cat.pack(source_pos, edge_rows, blob_members, sources_per_blob)
     catalogs = exchange(packed, zone_moves, None, lambda dz, db, z, b: z, zones, sizes, 0)
@@ -390,26 +489,27 @@
         in_specs=[SMEM, VMEM],
         out_specs=VMEM,
     )(codes, got)
-    shares = exchange(
-        totals.reshape(bands, share * ROWS, LANES),
-        band_moves, lambda z, b: b, lambda dz, db, z, b: b, bands, sizes, 2,
-    )
-    solved = pl.pallas_call(
-        solve_kernel,
-        out_shape=jax.ShapeDtypeStruct((-(-share // 8) * 8, LANES), jnp.float32),
-        in_specs=[VMEM],
+    near = 3 * bands - 1
+    seats = -(-share // 8) * 8
+    return pl.pallas_call(
+        functools.partial(finish_kernel, cat, zones, bands, share),
+        out_shape=jax.ShapeDtypeStruct((FILTER_BANDS, sources), jnp.float32),
+        in_specs=[VMEM, VMEM],
         out_specs=VMEM,
-    )(shares.reshape(bands, share, ROWS, LANES))
-    fluxes = exchange(
-        solved, near_moves, None, lambda dz, db, z, b: (1 - dz) * bands + b, 3 * bands, sizes, 3
-    )
-    return pl.pallas_call(
-        functools.partial(place_kernel, cat, zones, bands, share),
-        out_shape=jax.ShapeDtypeStruct((FILTER_BANDS, sources), jnp.float32),
-        in_specs=[SMEM, VMEM, VMEM],
-        out_specs=VMEM,
-        scratch_shapes=[pltpu.VMEM((sources, cat.member_rows * LANES), jnp.bfloat16)],
-    )(lax.axis_index("zone").reshape(1), catalogs, fluxes)
+        scratch_shapes=[
+            pltpu.VMEM((bands, share * ROWS, LANES), jnp.float32),
+            pltpu.VMEM((seats, LANES), jnp.float32),
+            pltpu.VMEM((3 * bands, seats, LANES), jnp.float32),
+            pltpu.VMEM((3, sources, cat.member_rows * LANES), jnp.bfloat16),
+            pltpu.SemaphoreType.DMA((bands - 1,)),
+            pltpu.SemaphoreType.DMA((bands - 1,)),
+            pltpu.SemaphoreType.DMA,
+            pltpu.SemaphoreType.DMA((near,)),
+            pltpu.SemaphoreType.DMA((near,)),
+            pltpu.SemaphoreType.DMA,
+        ],
+        compiler_params=pltpu.CompilerParams(collective_id=2, has_side_effects=True),
+    )(totals.reshape(bands, share * ROWS, LANES), catalogs)
 
 
 def solution(mesh):

time: 152 us -> 101 us (0.66)
  Pallas kernels: 143 us -> 91.3 us
    pallas_call x1, Pallas kernels: 91.4 us -> 45.4 us  [tile_terms(): pl.pallas_call(functools.partial(tile_kernel, cat, zones, groups), grid=(...]
    pallas_call x4 -> x2, Pallas kernels: 40.2 us -> 21.8 us  [exchange(): pl.pallas_call(kernel, out_shape=jax.ShapeDtypeStruct((slots,) + piece, b...]
    pallas_call x2 -> x1, Pallas kernels: 6.25 us -> 18.3 us  [on_device(): pl.pallas_call(functools.partial(finish_kernel, cat, zones, bands, share)...]
where the time goes in v2:
time: 101 us; the launch traced here: 100 us
  Pallas kernels  91.3 us (90%)
  local copies, waits for them, and re-layouts  5.02 us (5%)
  other arithmetic  3.89 us (4%)
    pallas_call x1, Pallas kernels, tile_terms(): pl.pallas_call(functools.partial(tile_kernel, cat, zones, groups), grid=(...  45.4 us
    pallas_call x2, Pallas kernels, exchange(): pl.pallas_call(kernel, out_shape=jax.ShapeDtypeStruct((slots,) + piece, b...  21.8 us
    pallas_call x1, Pallas kernels, on_device(): pl.pallas_call(functools.partial(finish_kernel, cat, zones, bands, share)...  18.3 us
    pallas_call x1, Pallas kernels, on_device(): pl.pallas_call(functools.partial(gather_kernel, capacity, groups), out_sh...  5.83 us

profile of v2, /device:TPU:0, one launch (start us, length us, event | category | flops | bytes accessed | tf_op | source)
XLA Modules:
  0.0 100.2 jit_solution(15218704522580998365)
XLA Ops:
  0.0 0.7 convert_bitcast_fusion
  0.7 0.7 convert_element_type.17
  1.3 1.3 %multiply_divide_fusion.spread_ref = f32[3,128]{1,0:T(4,128)} fusion(f32[3,128]{1,0:T(4,128)} %param.15), kind=kLoop, calls=%fused_computation | loop fusion | flops 768 | bytes 3072 | tf_op jit(solution)/shard_map/div | solution.py:476
  2.6 0.7 reshape.22
  3.3 0.7 convert_element_type.18
  4.0 0.1 copy.13
  4.1 0.1 reshape.25
  4.1 1.8 %concatenate.3.x_ref = f32[24,128]{1,0:T(8,128)} concatenate(f32[8,128]{1,0:T(8,128)S(1)} %reshape.22, f32[1,128]{1,0:T(1,128)S(1)} %convert_bitcast_fusion, f32[1,128]{1,0:T(1,128)S(1)} %pad_bitcast_fusion, f32[6,128]{1,0:T(8,128)S(1)} %broadcast_in_dim.3, f32[8,128]{1,0:T(8,128)S(1)} %reshape.25), dimensions={0} | concatenate | bytes 24576 | tf_op jit(solution)/shard_map/concatenate | solution.py:104
  5.9 10.3 %shard_map.109.cat_ref = f32[8,24,128]{2,1,0:T(8,128)} custom-call(f32[24,128]{1,0:T(8,128)} %concatenate.3.x_ref), custom_call_target="tpu_custom_call" | custom-call | tf_op jit(solution)/shard_map/pallas_call | solution.py:59
  16.2 45.4 %shard_map.110 = f32[32,24,128]{2,1,0:T(8,128)} custom-call(s32[128]{0:T(128)} %blob_ref.1, s32[128]{0:T(128)} %band_ref.1, f32[2,128]{1,0:T(2,128)} %shift_ref.1, f32[3,128]{1,0:T(4,128)} %amp_ref.1, f32[3,128]{1,0:T(4,128)} %multiply_divide_fusion.spread_ref, f32[8,24,128]{2,1,0:T(8,128)} %shard_map.109.cat_ref, f32[128,32,128]{2,1,0:T(8,128)} %pixel_ref.1, ...), custom_call_target="tpu_custom_call" | custom-call | tf_op jit(solution)/shard_map/pallas_call | solution.py:300
  61.6 11.6 %shard_map.111 = f32[8,96,128]{2,1,0:T(8,128)} custom-call(f32[8,96,128]{2,1,0:T(8,128)} %bitcast.10), custom_call_target="tpu_custom_call" | custom-call | tf_op jit(solution)/shard_map/pallas_call | solution.py:59
  73.2 1.1 %slice.3 = f32[32,1,8]{2,1,0:T(1,128)S(1)} slice(f32[32,24,128]{2,1,0:T(8,128)} %bitcast.8), slice={[0:32:1], [17:18:1], [0:128:16]} | slice | bytes 2048 | tf_op jit(solution)/shard_map/slice | solution.py:485
  74.2 0.6 convert_element_type.19
  74.8 5.8 %shard_map.112 = f32[24,24,128]{2,1,0:T(8,128)} custom-call(s32[32,8]{1,0:T(8,128)} %bitcast.12, f32[32,24,128]{2,1,0:T(8,128)} %bitcast.9), custom_call_target="tpu_custom_call" | custom-call | tf_op jit(solution)/shard_map/pallas_call | solution.py:486
  80.7 18.3 %shard_map.113 = f32[3,512]{1,0:T(4,128)} custom-call(f32[4,144,128]{2,1,0:T(8,128)} %bitcast.11, f32[8,24,128]{2,1,0:T(8,128)} %shard_map.109.cat_ref), custom_call_target="tpu_custom_call" | custom-call | tf_op jit(solution)/shard_map/pallas_call | solution.py:494
  98.9 1.3 %copy.15 = f32[3,512]{1,0:T(4,128)} copy(f32[3,512]{1,0:T(4,128)} %shard_map.113) | data formatting | bytes 12288
  (2 shorter events, 0.0 us)

commit v3 on v2

--- a/solution.py
+++ b/solution.py
@@ -14,17 +14,19 @@
 PACK = LANES // MAX_SOURCES
 ROWS = 24
 TILES_STEP = 4
+CHUNK = 8
 PRIOR = 1.0
 
 VMEM = pl.BlockSpec(memory_space=pltpu.VMEM)
 SMEM = pl.BlockSpec(memory_space=pltpu.SMEM)
 
 
-def exchange(block, moves, pick, slot, slots, sizes, ident):
+def exchange(block, moves, pick, slot, slots, sizes, ident, label_row=None):
     zones, bands = sizes
     piece = block.shape[-2:] if pick is None else block.shape[1:]
 
-    def kernel(x_ref, o_ref, send_sem, recv_sem, own_sem):
+    def kernel(x_ref, o_ref, *refs):
+        send_sem, recv_sem, own_sem = refs[-3:]
         zone = lax.axis_index("zone")
         band = lax.axis_index("band")
         targets = [
@@ -55,12 +57,23 @@
         own.wait()
         for copy in copies:
             copy.wait()
-
+        if label_row is not None:
+            code_ref = refs[0]
+            groups = piece[0] // ROWS
+            for order in range(slots * groups):
+                at = order % groups * ROWS + label_row
+                code_ref[order : order + 1, :] = o_ref[order // groups, at : at + 1, :].astype(
+                    jnp.int32
+                )
+
+    out_shape = [jax.ShapeDtypeStruct((slots,) + piece, block.dtype)]
+    if label_row is not None:
+        out_shape.append(jax.ShapeDtypeStruct((slots * piece[0] // ROWS, LANES), jnp.int32))
     return pl.pallas_call(
         kernel,
-        out_shape=jax.ShapeDtypeStruct((slots,) + piece, block.dtype),
+        out_shape=out_shape,
         in_specs=[VMEM],
-        out_specs=VMEM,
+        out_specs=[VMEM] * len(out_shape),
         scratch_shapes=[
             pltpu.SemaphoreType.DMA((len(moves),)),
             pltpu.SemaphoreType.DMA((len(moves),)),
@@ -93,15 +106,27 @@
         self.rows = self.member_row + -(-self.member_rows // 8) * 8
         self.sources, self.edge, self.blobs = sources, edge, blobs
 
-    def pack(self, source_pos, edge_rows, blob_members, counts):
-        pieces = [
-            source_pos.reshape(-1, LANES),
-            edge_rows.astype(jnp.float32).reshape(1, LANES),
-            jnp.pad(counts.astype(jnp.float32), (0, LANES - counts.shape[0])).reshape(1, LANES),
-            jnp.zeros((self.member_row - self.count_row - 1, LANES), jnp.float32),
-            blob_members.astype(jnp.float32).reshape(-1, LANES),
+    def pack(self, source_ref, edge_ref, member_ref, count_ref, sigma_ref, out_ref, spread_ref):
+        out_ref[...] = jnp.zeros_like(out_ref)
+        for coord in range(2):
+            for part in range(self.parts):
+                at = coord * self.parts + part
+                out_ref[at : at + 1, :] = source_ref[
+                    coord : coord + 1, part * LANES : (part + 1) * LANES
+                ]
+        out_ref[self.edge_row : self.edge_row + 1, :] = edge_ref[...].astype(jnp.float32)
+        out_ref[self.count_row : self.count_row + 1, : self.blobs] = count_ref[...].astype(
+            jnp.float32
+        )
+        seats = [
+            member_ref[pl.ds(seat, self.member_rows, stride=PACK), :].astype(jnp.float32)
+            for seat in range(PACK)
         ]
-        return jnp.concatenate(pieces, axis=0)
+        out_ref[self.member_row : self.member_row + self.member_rows, :] = jnp.concatenate(
+            seats, axis=1
+        )
+        sigma = sigma_ref[...]
+        spread_ref[...] = 0.5 / (sigma * sigma)
 
     def members(self, ref, zone):
         return ref[zone, self.member_row : self.member_row + self.member_rows, :].astype(jnp.int32)
@@ -161,7 +186,7 @@
     cat, zones, groups,
     blob_ref, band_ref, shift_ref, amp_ref, spread_ref,
     cat_ref, pixel_ref, weight_ref,
-    out_ref, edge_ref, table_ref, factor_ref, line_ref, used_ref,
+    out_ref, edge_ref, table_ref, line_ref, used_ref,
 ):
     step = pl.program_id(0)
     height = pixel_ref.shape[1]
@@ -215,7 +240,7 @@
         line_ref[slot, 0] = root
         line_ref[slot, 1] = image_head
         line_ref[slot, 2] = image - image_head
-        models = []
+        rights = []
         for h in range(2):
             index = offset + h * half + eight_lane % half
             row_pos = jnp.take_along_axis(table[0][:8], index, axis=1, mode="promise_in_bounds")
@@ -228,48 +253,68 @@
             )
             span = slice(h * half, (h + 1) * half)
             heads = [c[span] for c in cols_head]
-            right = jnp.concatenate(
-                heads + heads + [c[span] for c in cols_tail] + [blank], axis=0
-            ).astype(jnp.bfloat16)
-            left = []
-            for i in range(0, height, 2):
-                pair = jnp.concatenate(
-                    [
-                        jnp.broadcast_to(line_ref[slot, 3 + h, i + d : i + d + 1, :], (half, LANES))
-                        for d in range(2)
-                    ],
-                    axis=0,
+            rights.append(
+                jnp.concatenate(
+                    heads + heads + [c[span] for c in cols_tail] + [blank], axis=0
+                ).astype(jnp.bfloat16)
+            )
+
+        def render(chunk):
+            models = []
+            for h in range(2):
+                left = []
+                for i in range(chunk * CHUNK, (chunk + 1) * CHUNK, 2):
+                    pair = jnp.concatenate(
+                        [
+                            jnp.broadcast_to(
+                                line_ref[slot, 3 + h, i + d : i + d + 1, :], (half, LANES)
+                            )
+                            for d in range(2)
+                        ],
+                        axis=0,
+                    )
+                    left.append(jnp.where(keep, pair, 0.0).astype(jnp.bfloat16))
+                models.append(
+                    lax.dot_general(
+                        jnp.concatenate(left, axis=0), rights[h], (((1,), (0,)), ((), ())),
+                        preferred_element_type=jnp.float32,
+                    )
                 )
-                left.append(jnp.where(keep, pair, 0.0).astype(jnp.bfloat16))
-            models.append(
-                lax.dot_general(
-                    jnp.concatenate(left, axis=0), right, (((1,), (0,)), ((), ())),
-                    preferred_element_type=jnp.float32,
+            return models
+
+        product = None
+        chunks = height // CHUNK
+        ahead = render(0)
+        for chunk in range(chunks):
+            models = ahead
+            if chunk + 1 < chunks:
+                ahead = render(chunk + 1)
+            heads, tails, lines = [], [], []
+            for at_row in range(CHUNK):
+                i = chunk * CHUNK + at_row
+                span = slice(at_row * half, (at_row + 1) * half)
+                weight = jnp.broadcast_to(line_ref[slot, 0, i : i + 1, :], shape)
+                scaled = jnp.concatenate([models[0][span], models[1][span]], axis=0) * weight
+                head = scaled.astype(jnp.bfloat16)
+                heads.append(head)
+                tails.append((scaled - head.astype(jnp.float32)).astype(jnp.bfloat16))
+                lines.append(
+                    jnp.concatenate(
+                        [
+                            jnp.broadcast_to(line_ref[slot, k, i : i + 1, :], (half, LANES))
+                            for k in (1, 2)
+                        ],
+                        axis=0,
+                    ).astype(jnp.bfloat16)
                 )
-            )
-        for i in range(height):
-            span = slice(i * half, (i + 1) * half)
-            weight = jnp.broadcast_to(line_ref[slot, 0, i : i + 1, :], shape)
-            scaled = jnp.concatenate([models[0][span], models[1][span]], axis=0) * weight
-            head = scaled.astype(jnp.bfloat16)
-            tail = (scaled - head.astype(jnp.float32)).astype(jnp.bfloat16)
-            seen = jnp.concatenate(
-                [
-                    jnp.broadcast_to(line_ref[slot, k, i : i + 1, :], (half, LANES))
-                    for k in (1, 2)
-                ],
-                axis=0,
-            ).astype(jnp.bfloat16)
-            where = slice(i * LANES, (i + 1) * LANES)
-            factor_ref[slot, 0:16, where] = head
-            factor_ref[slot, 16:32, where] = tail
-            factor_ref[slot, 32:48, where] = seen
-        product = lax.dot_general(
-            factor_ref[slot],
-            factor_ref[slot, 0:32, :],
-            (((1,), (1,)), ((), ())),
-            preferred_element_type=jnp.float32,
-        )
+            factor = jnp.concatenate(
+                [jnp.concatenate(heads, axis=1), jnp.concatenate(tails, axis=1)], axis=0
+            )
+            left = jnp.concatenate([factor, jnp.concatenate(lines, axis=1)], axis=0)
+            part = lax.dot_general(
+                left, factor, (((1,), (1,)), ((), ())), preferred_element_type=jnp.float32
+            )
+            product = part if product is None else product + part
         folded = product[:, :16] + product[:, 16:]
         normal = folded[:16] + folded[16:32]
         vector = folded[32:40] + folded[40:48]
@@ -306,7 +351,6 @@
         scratch_shapes=[
             pltpu.VMEM((2, zones, 8, LANES), jnp.float32),
             pltpu.VMEM((3, zones * cat.member_rows, LANES), jnp.float32),
-            pltpu.VMEM((per, 48, height * width), jnp.bfloat16),
             pltpu.VMEM((per, 5, height, width), jnp.float32),
             pltpu.SMEM((zones,), jnp.int32),
         ],
@@ -321,7 +365,7 @@
     def body(group, carry):
         block = got_ref[group]
         for seat in range(min(PACK, capacity)):
-            code = code_ref[group, seat]
+            code = code_ref[group, seat * MAX_SOURCES]
             to = code % PACK
             moved = pltpu.roll(block, ((to - seat + PACK) % PACK) * MAX_SOURCES, 1)
             place = code // PACK
@@ -471,18 +515,29 @@
     share = systems // bands
     zone_moves = [(d, 0) for d in range(1, zones)]
 
-    packed = cat.pack(source_pos, edge_rows, blob_members, sources_per_blob)
-    catalogs = exchange(packed, zone_moves, None, lambda dz, db, z, b: z, zones, sizes, 0)
-    spread = 0.5 / (psf_sigma * psf_sigma)
+    packed, spread = pl.pallas_call(
+        cat.pack,
+        out_shape=(
+            jax.ShapeDtypeStruct((cat.rows, LANES), jnp.float32),
+            jax.ShapeDtypeStruct(psf_sigma.shape, jnp.float32),
+        ),
+        in_specs=[VMEM] * 5,
+        out_specs=(VMEM, VMEM),
+    )(
+        source_pos, edge_rows.reshape(1, -1), blob_members, sources_per_blob.reshape(1, -1),
+        psf_sigma,
+    )
+    (catalogs,) = exchange(packed, zone_moves, None, lambda dz, db, z, b: z, zones, sizes, 0)
     terms = tile_terms(
         cat, zones, groups, tile_blob, tile_band, tile_offset, psf_amp, spread, catalogs,
         pixels, inv_var,
     )
-    got = exchange(
+    got, codes = exchange(
         terms.reshape(zones, groups * ROWS, LANES),
         zone_moves, lambda z, b: z, lambda dz, db, z, b: z, zones, sizes, 1,
-    ).reshape(zones * groups, ROWS, LANES)
-    codes = got[:, MAX_SOURCES + 1, ::MAX_SOURCES].astype(jnp.int32)
+        MAX_SOURCES + 1,
+    )
+    got = got.reshape(zones * groups, ROWS, LANES)
     totals = pl.pallas_call(
         functools.partial(gather_kernel, capacity, groups),
         out_shape=jax.ShapeDtypeStruct((systems, ROWS, LANES), jnp.float32),

time: 101 us -> 99.5 us (0.985)
  Pallas kernels: 91.3 us -> 96.4 us
  other arithmetic: 3.89 us -> 0 us
  local copies, waits for them, and re-layouts: 5.02 us -> 2.68 us
    pallas_call x1, Pallas kernels: 45.4 us -> 48.8 us  [tile_terms(): pl.pallas_call(functools.partial(tile_kernel, cat, zones, groups), grid=(...]
    convert_element_type x3 -> x0, other arithmetic: 1.97 us -> none  [the longest x1 0.7 us: pack(): blob_members.astype(jnp.float32).reshape(-1, LANES)]
    concatenate x1 -> x0, local copies, waits for them, and re-layouts: 1.79 us -> none  [pack(): return jnp.concatenate(pieces, axis=0)]
    pallas_call x2 -> x3, Pallas kernels: 21.8 us -> 23.3 us  [the longest x2 21.9 us: exchange(): pl.pallas_call(kernel, out_shape=out_shape, in_specs=[VMEM], out_specs=[V...]
    unnamed x1 -> x2, local copies, waits for them, and re-layouts: 1.3 us -> 2.68 us
    div x1 -> x0, other arithmetic: 1.27 us -> none  [on_device(): spread = 0.5 / (psf_sigma * psf_sigma)]
    slice x1 -> x0, local copies, waits for them, and re-layouts: 1.06 us -> none  [on_device(): codes = got[:, MAX_SOURCES + 1, ::MAX_SOURCES].astype(jnp.int32)]
where the time goes in v3:
time: 99.5 us; the launch traced here: 99.1 us
  Pallas kernels  96.4 us (97%)
  local copies, waits for them, and re-layouts  2.68 us (3%)
    pallas_call x1, Pallas kernels, tile_terms(): pl.pallas_call(functools.partial(tile_kernel, cat, zones, groups), grid=(...  48.8 us
    pallas_call x2, Pallas kernels, exchange(): pl.pallas_call(kernel, out_shape=out_shape, in_specs=[VMEM], out_specs=[V...  21.9 us
    pallas_call x1, Pallas kernels, on_device(): pl.pallas_call(functools.partial(finish_kernel, cat, zones, bands, share)...  18.5 us
    pallas_call x1, Pallas kernels, on_device(): pl.pallas_call(functools.partial(gather_kernel, capacity, groups), out_sh...  5.8 us
    unnamed x2, local copies, waits for them, and re-layouts  2.68 us

profile of v3, /device:TPU:0, one launch (start us, length us, event | category | flops | bytes accessed | tf_op | source)
XLA Modules:
  0.0 99.1 jit_solution(17862408249429657262)
XLA Ops:
  0.0 1.4 %copy.12.member_ref = s32[64,16]{1,0:T(8,128)} copy(s32[64,16]{0,1:T(8,128)} %param.20) | data formatting | bytes 8192 | tf_op args[9]
  1.4 1.5 %shard_map.109 = (f32[24,128]{1,0:T(8,128)}, f32[3,128]{1,0:T(4,128)}) custom-call(f32[2,512]{1,0:T(2,128)} %source_ref.1, s32[1,128]{1,0:T(1,128)} %bitcast.8, s32[64,16]{1,0:T(8,128)} %copy.12.member_ref, s32[1,64]{1,0:T(1,128)} %bitcast.9, f32[3,128]{1,0:T(4,128)} %sigma_ref.1), custom_call_target="tpu_custom_call" | custom-call | tf_op jit(solution)/shard_map/pallas_call | solution.py:518
  2.9 10.3 %shard_map.110.cat_ref = f32[8,24,128]{2,1,0:T(8,128)} custom-call(f32[24,128]{1,0:T(8,128)} %get-tuple-element.10.x_ref), custom_call_target="tpu_custom_call" | custom-call | tf_op jit(solution)/shard_map/pallas_call | solution.py:72
  13.2 48.8 %shard_map.111 = f32[32,24,128]{2,1,0:T(8,128)} custom-call(s32[128]{0:T(128)} %blob_ref.1, s32[128]{0:T(128)} %band_ref.1, f32[2,128]{1,0:T(2,128)} %shift_ref.1, f32[3,128]{1,0:T(4,128)} %amp_ref.1, f32[3,128]{1,0:T(4,128)} %get-tuple-element.9.spread_ref, f32[8,24,128]{2,1,0:T(8,128)} %shard_map.110.cat_ref, f32[128,32,128]{2,1,0:T(8,128)} %pixel_ref.1, ...), custom_call_target="tpu_custom_call" | custom-call | tf_op jit(solution)/shard_map/pallas_call | solution.py:345
  61.9 11.6 %shard_map.112 = (f32[8,96,128]{2,1,0:T(8,128)}, s32[32,128]{1,0:T(8,128)}) custom-call(f32[8,96,128]{2,1,0:T(8,128)} %bitcast.5), custom_call_target="tpu_custom_call" | custom-call | tf_op jit(solution)/shard_map/pallas_call | solution.py:72
  73.5 5.8 %shard_map.113 = f32[24,24,128]{2,1,0:T(8,128)} custom-call(s32[32,128]{1,0:T(8,128)} %get-tuple-element.11.code_ref, f32[32,24,128]{2,1,0:T(8,128)} %bitcast.7), custom_call_target="tpu_custom_call" | custom-call | tf_op jit(solution)/shard_map/pallas_call | solution.py:541
  79.3 18.5 %shard_map.114 = f32[3,512]{1,0:T(4,128)} custom-call(f32[4,144,128]{2,1,0:T(8,128)} %bitcast.6, f32[8,24,128]{2,1,0:T(8,128)} %shard_map.110.cat_ref), custom_call_target="tpu_custom_call" | custom-call | tf_op jit(solution)/shard_map/pallas_call | solution.py:549
  97.8 1.3 %copy.14 = f32[3,512]{1,0:T(4,128)} copy(f32[3,512]{1,0:T(4,128)} %shard_map.114) | data formatting | bytes 12288

commit v4 on v3

--- a/solution.py
+++ b/solution.py
@@ -13,8 +13,8 @@
 LANES = 128
 PACK = LANES // MAX_SOURCES
 ROWS = 24
-TILES_STEP = 4
-CHUNK = 8
+TILES_STEP = 16
+CHUNK = 32
 PRIOR = 1.0
 
 VMEM = pl.BlockSpec(memory_space=pltpu.VMEM)

time: 99.5 us -> 83.3 us (0.84)
  Pallas kernels: 96.4 us -> 80.1 us
    pallas_call x1, Pallas kernels: 48.8 us -> 32.7 us  [tile_terms(): pl.pallas_call(functools.partial(tile_kernel, cat, zones, groups), grid=(...]
where the time goes in v4:
time: 83.3 us; the launch traced here: 82.8 us
  Pallas kernels  80.1 us (96%)
  local copies, waits for them, and re-layouts  2.68 us (3%)
    pallas_call x1, Pallas kernels, tile_terms(): pl.pallas_call(functools.partial(tile_kernel, cat, zones, groups), grid=(...  32.7 us
    pallas_call x2, Pallas kernels, exchange(): pl.pallas_call(kernel, out_shape=out_shape, in_specs=[VMEM], out_specs=[V...  21.9 us
    pallas_call x1, Pallas kernels, on_device(): pl.pallas_call(functools.partial(finish_kernel, cat, zones, bands, share)...  18.2 us
    pallas_call x1, Pallas kernels, on_device(): pl.pallas_call(functools.partial(gather_kernel, capacity, groups), out_sh...  5.83 us
    unnamed x2, local copies, waits for them, and re-layouts  2.68 us

profile of v4, /device:TPU:0, one launch (start us, length us, event | category | flops | bytes accessed | tf_op | source)
XLA Modules:
  0.0 82.8 jit_solution(13189925229444331367)
XLA Ops:
  0.0 1.4 %copy.12.member_ref = s32[64,16]{1,0:T(8,128)} copy(s32[64,16]{0,1:T(8,128)} %param.20) | data formatting | bytes 8192 | tf_op args[9]
  1.4 1.5 %shard_map.109 = (f32[24,128]{1,0:T(8,128)}, f32[3,128]{1,0:T(4,128)}) custom-call(f32[2,512]{1,0:T(2,128)} %source_ref.1, s32[1,128]{1,0:T(1,128)} %bitcast.8, s32[64,16]{1,0:T(8,128)} %copy.12.member_ref, s32[1,64]{1,0:T(1,128)} %bitcast.9, f32[3,128]{1,0:T(4,128)} %sigma_ref.1), custom_call_target="tpu_custom_call" | custom-call | tf_op jit(solution)/shard_map/pallas_call | solution.py:518
  2.9 10.3 %shard_map.110.cat_ref = f32[8,24,128]{2,1,0:T(8,128)} custom-call(f32[24,128]{1,0:T(8,128)} %get-tuple-element.10.x_ref), custom_call_target="tpu_custom_call" | custom-call | tf_op jit(solution)/shard_map/pallas_call | solution.py:72
  13.2 32.7 %shard_map.111 = f32[32,24,128]{2,1,0:T(8,128)} custom-call(s32[128]{0:T(128)} %blob_ref.1, s32[128]{0:T(128)} %band_ref.1, f32[2,128]{1,0:T(2,128)} %shift_ref.1, f32[3,128]{1,0:T(4,128)} %amp_ref.1, f32[3,128]{1,0:T(4,128)} %get-tuple-element.9.spread_ref, f32[8,24,128]{2,1,0:T(8,128)} %shard_map.110.cat_ref, f32[128,32,128]{2,1,0:T(8,128)} %pixel_ref.1, ...), custom_call_target="tpu_custom_call" | custom-call | tf_op jit(solution)/shard_map/pallas_call | solution.py:345
  45.8 11.6 %shard_map.112 = (f32[8,96,128]{2,1,0:T(8,128)}, s32[32,128]{1,0:T(8,128)}) custom-call(f32[8,96,128]{2,1,0:T(8,128)} %bitcast.5), custom_call_target="tpu_custom_call" | custom-call | tf_op jit(solution)/shard_map/pallas_call | solution.py:72
  57.4 5.8 %shard_map.113 = f32[24,24,128]{2,1,0:T(8,128)} custom-call(s32[32,128]{1,0:T(8,128)} %get-tuple-element.11.code_ref, f32[32,24,128]{2,1,0:T(8,128)} %bitcast.7), custom_call_target="tpu_custom_call" | custom-call | tf_op jit(solution)/shard_map/pallas_call | solution.py:541
  63.2 18.2 %shard_map.114 = f32[3,512]{1,0:T(4,128)} custom-call(f32[4,144,128]{2,1,0:T(8,128)} %bitcast.6, f32[8,24,128]{2,1,0:T(8,128)} %shard_map.110.cat_ref), custom_call_target="tpu_custom_call" | custom-call | tf_op jit(solution)/shard_map/pallas_call | solution.py:549
  81.5 1.3 %copy.14 = f32[3,512]{1,0:T(4,128)} copy(f32[3,512]{1,0:T(4,128)} %shard_map.114) | data formatting | bytes 12288
